TPU v7x, 32 devices: a whole 2x2x4 slice. The times are simulated.
32 devices in a mesh: expert: 8 (over y, x, core), dp: 4 (over z).
Axes of the slice: x: 2, y: 2, z: 4, core: 2. Of those that a mesh axis runs over, the one named last changes fastest.
Arguments:
- trunk: bfloat16 [768, 4096], P(('dp', 'expert')), may hold values from -6 to 6
- w_first: bfloat16 [8, 4096, 2048], P('expert'), may hold values from -0.09375 to 0.09375
- w_second: bfloat16 [8, 2048, 1024], P('expert'), may hold values from -0.125 to 0.125
- gates: bfloat16 [8, 8, 768], P('expert', None, 'dp'), may hold values from 0.049804688 to 1
- d_mixed: bfloat16 [768, 8, 1024], P(('dp', 'expert')), may hold values from -6 to 6
Outputs:
- mixed: bfloat16 [768, 8, 1024], P(('dp', 'expert'))
- d_trunk: bfloat16 [768, 4096], P(('dp', 'expert'))
- d_gates: bfloat16 [8, 8, 768], P('expert', None, 'dp')
- d_w_first: bfloat16 [8, 4096, 2048], P('expert', 'dp')
- d_w_second: bfloat16 [8, 2048, 1024], P('expert', 'dp')
All inputs are finite; a program needn't handle non-finite values.
Results may differ from a plain program's by a relative error of at most 0.015.
Values may be sent and summed in bfloat16 or wider, within the bound.
A program may use at most 128 MiB of HBM per device.

v0:
```python
import jax
import jax.numpy as jnp
from jax import lax
from jax.sharding import PartitionSpec as P

F32 = jnp.float32
BF16 = jnp.bfloat16


def on_device(trunk, w_first, w_second, gates, d_mixed):
    rank = lax.axis_index("dp")
    first = w_first[0]
    second = w_second[0]
    gate_here = gates[0]
    n_dp = lax.axis_size("dp")
    depth = first.shape[0] // n_dp
    units = second.shape[0] // n_dp
    group = gate_here.shape[1]
    rows_all = lax.all_gather(trunk, ("dp", "expert"), axis=0, tiled=True)
    gates_each = lax.all_to_all(
        gate_here.T[None], "expert", split_axis=1, concat_axis=0, tiled=True
    )
    d_out_each = jnp.einsum("ert,rto->ero", gates_each, d_mixed, preferred_element_type=F32).astype(
        BF16
    )
    d_output = lax.all_to_all(d_out_each, "expert", split_axis=0, concat_axis=1, tiled=True)[0]
    d_output_all = lax.all_gather(d_output, "dp", axis=0, tiled=True)
    pre = jnp.dot(rows_all, first, preferred_element_type=F32)
    pre_here = lax.dynamic_slice_in_dim(pre, rank * group, group, 0)
    hidden_here = jax.nn.silu(pre_here).astype(BF16)
    output = jnp.dot(hidden_here, second, preferred_element_type=F32).astype(BF16)
    outs_each = lax.all_to_all(output[None], "expert", split_axis=1, concat_axis=0, tiled=True)
    d_hidden = lax.dot_general(
        d_output_all, second, (((1,), (1,)), ((), ())), preferred_element_type=F32
    )
    sig = jax.nn.sigmoid(pre)
    d_pre = (d_hidden * sig * (1.0 + pre * (1.0 - sig))).astype(BF16)
    d_pre_here = lax.dynamic_slice_in_dim(d_pre, rank * group, group, 0)
    d_trunk = lax.psum_scatter(
        lax.dot_general(
            d_pre_here, first, (((1,), (1,)), ((), ())), preferred_element_type=F32
        ).astype(BF16),
        "expert",
        scatter_dimension=0,
        tiled=True,
    )
    mixed = jnp.einsum("ert,ero->rto", gates_each, outs_each, preferred_element_type=F32).astype(
        BF16
    )
    d_gate_each = jnp.einsum("rto,ero->ert", d_mixed, outs_each, preferred_element_type=F32).astype(
        BF16
    )
    back_gate = lax.all_to_all(d_gate_each, "expert", split_axis=0, concat_axis=1, tiled=True)
    d_gate = back_gate[0].T[None]
    columns = lax.dynamic_slice_in_dim(rows_all, rank * depth, depth, 1)
    d_first = lax.dot_general(
        columns, d_pre, (((0,), (0,)), ((), ())), preferred_element_type=F32
    ).astype(BF16)
    some_pre = lax.dynamic_slice_in_dim(pre, rank * units, units, 1)
    some_hidden = jax.nn.silu(some_pre).astype(BF16)
    d_second = lax.dot_general(
        some_hidden, d_output_all, (((0,), (0,)), ((), ())), preferred_element_type=F32
    ).astype(BF16)
    return (mixed, d_trunk, d_gate, d_first[None], d_second[None])


def solution(mesh):
    in_specs = (
        P(("dp", "expert"), None),
        P("expert", None, None),
        P("expert", None, None),
        P("expert", None, "dp"),
        P(("dp", "expert"), None, None),
    )
    out_specs = (
        P(("dp", "expert"), None, None),
        P(("dp", "expert"), None),
        P("expert", None, "dp"),
        P("expert", "dp", None),
        P("expert", "dp", None),
    )
    return jax.shard_map(
        on_device, mesh=mesh, in_specs=in_specs, out_specs=out_specs, check_vma=False
    )
```

profile of v0, /device:TPU:0, one launch (start us, length us, event | category | flops | bytes accessed | tf_op | source)
XLA Modules:
  0.0 188.0 jit_solution(14458525638862660231)
XLA Ops:
  7.2 0.0 copy-start
  7.2 0.0 all-gather.3.cloned.1.call-start
  7.2 0.7 all-gather.3.cloned.1.call-update
  7.9 0.8 copy.28
  8.7 10.2 %all_to_all.42 = bf16[1,192,8]{2,0,1:T(2,128)(2,1)S(1)} all-to-all(bf16[1,192,8]{2,0,1:T(2,128)(2,1)S(1)} %copy.28), channel_id=1, replica_groups=mesh['expert'=8,'dp'=4] {'expert'}, dimensions={1} | all-to-all | bytes 6144 | tf_op jit(solution)/shard_map/all_to_all | solution.py:20
  18.9 0.1 copy.29
  19.0 0.1 all_to_all.15
  19.1 0.1 copy.32
  19.2 0.0 copy-done
  19.2 0.2 fusion.19
  19.5 1.0 copy.33
  20.5 3.5 %all-to-all-start.2 = ((bf16[8,24,1024]{2,1,0:T(8,128)(2,1)}), bf16[8,24,1024]{2,1,0:T(8,128)(2,1)S(1)}, u32[]{:S(2)}, u32[]{:S(2)}) async-start(bf16[8,24,1024]{2,1,0:T(8,128)(2,1)} %copy.33), calls=%async_computation.2 | async-start | bytes 786432 | tf_op jit(solution)/shard_map/all_to_all | solution.py:26
  23.9 0.0 all-gather.5.cloned.1.call-start
  24.0 8.2 %all-to-all-done.2 = bf16[8,24,1024]{2,1,0:T(8,128)(2,1)S(1)} async-done(((bf16[8,24,1024]{2,1,0:T(8,128)(2,1)}), bf16[8,24,1024]{2,1,0:T(8,128)(2,1)S(1)}, u32[]{:S(2)}, u32[]{:S(2)}) %all-to-all-start.2) | async-done | bytes 393248 | tf_op jit(solution)/shard_map/all_to_all | solution.py:26
  32.2 0.0 copy-start.1
  32.2 0.7 copy-done.1
  32.9 0.0 all-gather.5.cloned.1.call-update
  32.9 0.0 reduce-scatter.2.cloned.1.call-start
  33.0 49.8 %all-gather.3.cloned.1.call-done = bf16[768,4096]{1,0:T(8,128)(2,1)} async-done(((bf16[24,4096]{1,0:T(8,128)(2,1)}), bf16[768,4096]{1,0:T(8,128)(2,1)}) %all-gather.3.cloned.1.call-update) | async-done | bytes 6291472 | tf_op jit(solution)/shard_map/all_gather | solution.py:19
  82.8 20.2 %fusion.2 = f32[768,2048]{1,0:T(8,128)} fusion(bf16[768,4096]{1,0:T(8,128)(2,1)} %all-gather.3.cloned.1.call-done, bf16[1,4096,2048]{2,1,0:T(8,128)(2,1)} %param.6), kind=kOutput, calls=%fused_computation.2 | convolution fusion | flops 12884901888 | bytes 29360128 | tf_op jit(solution)/shard_map/dot_general | solution.py:28
  103.0 17.5 %all-gather.5.cloned.1.call-done = bf16[768,1024]{1,0:T(8,128)(2,1)} async-done(((bf16[192,1024]{1,0:T(8,128)(2,1)}), bf16[768,1024]{1,0:T(8,128)(2,1)}) %all-gather.5.cloned.1.call-update) | async-done | bytes 1572880 | tf_op jit(solution)/shard_map/all_gather | solution.py:27
  120.5 10.8 %multiply_convert_fusion = bf16[768,2048]{1,0:T(8,128)(2,1)} fusion(f32[768,2048]{1,0:T(8,128)} %fusion.2, bf16[768,1024]{1,0:T(8,128)(2,1)} %all-gather.5.cloned.1.call-done, bf16[1,2048,1024]{2,1,0:T(8,128)(2,1)} %param.7), kind=kOutput, calls=%fused_computation.4 | convolution fusion | flops 3235381248 | bytes 15204352 | tf_op jit(solution)/shard_map/dot_general | solution.py:33
  131.3 12.8 %fusion.4 = bf16[192,4096]{1,0:T(8,128)(2,1)} fusion(bf16[1,4096,2048]{2,1,0:T(8,128)(2,1)} %param.6, bf16[768,2048]{1,0:T(8,128)(2,1)} %multiply_convert_fusion, s32[]{:T(128)S(6)} %select_n.10), kind=kOutput, calls=%fused_computation.5 | convolution fusion | flops 3222011904 | bytes 19136516 | tf_op jit(solution)/shard_map/dot_general | solution.py:40
  144.1 0.0 reduce-scatter.2.cloned.1.call-update
  144.1 3.7 %fusion.20 = bf16[1,192,1024]{2,1,0:T(8,128)(2,1)S(1)} fusion(bf16[1,2048,1024]{2,1,0:T(8,128)(2,1)} %param.7, f32[768,2048]{1,0:T(8,128)} %fusion.2, s32[]{:T(128)S(6)} %select_n.10), kind=kOutput, calls=%fused_computation.21 | convolution fusion | flops 807469056 | bytes 6160388 | tf_op jit(solution)/shard_map/dot_general | solution.py:31
  147.8 0.6 copy.43
  148.4 0.5 broadcast.9
  148.9 2.9 %reduce = bf16[192,1024]{1,0:T(8,128)(2,1)S(1)} reduce(bf16[192,1,1024]{2,1,0:T(2,128)(2,1)S(1)} %bitcast.56, bf16[]{:T(256)} %broadcast.9), dimensions={1}, to_apply=%bitcast.55.reduce_sub_computation | reduce | bytes 786434
  151.9 1.2 reshape.24
  153.1 3.6 %all-to-all-start = ((bf16[8,2,12288]{2,1,0:T(2,128)(2,1)}), bf16[8,2,12288]{2,1,0:T(2,128)(2,1)S(1)}, u32[]{:S(2)}, u32[]{:S(2)}) async-start(bf16[8,2,12288]{2,1,0:T(2,128)(2,1)} %reshape.24), calls=%async_computation | async-start | bytes 786432 | tf_op jit(solution)/shard_map/all_to_all | solution.py:32
  156.7 0.0 copy-start.2
  156.7 8.0 %convert_bitcast_fusion = bf16[1,1024,2048]{2,1,0:T(8,128)(2,1)} fusion(bf16[768,2048]{1,0:T(8,128)(2,1)} %multiply_convert_fusion, bf16[768,4096]{1,0:T(8,128)(2,1)} %all-gather.3.cloned.1.call-done, s32[]{:T(128)S(6)} %select_n.11), kind=kOutput, calls=%fused_computation.10 | convolution fusion | flops 3223322624 | bytes 8912900 | tf_op jit(solution)/shard_map/dot_general | solution.py:56
  164.7 0.0 copy-done.2
  164.7 3.4 %fusion.14 = bf16[1,512,1024]{2,1,0:T(8,128)(2,1)} fusion(bf16[768,1024]{1,0:T(8,128)(2,1)S(1)} %copy-done.2, f32[768,2048]{1,0:T(8,128)} %fusion.2, s32[]{:T(128)S(6)} %select_n.12), kind=kOutput, calls=%fused_computation.15 | convolution fusion | flops 807796736 | bytes 4194308 | tf_op jit(solution)/shard_map/dot_general | solution.py:61
  168.2 0.0 all-to-all-done
  168.2 0.4 reshape.25
  168.6 0.1 copy.37
  168.7 0.4 fusion.23
  169.1 0.7 copy.35
  169.8 4.2 %all-to-all-start.3 = ((bf16[8,24,8]{1,2,0:T(8,128)(2,1)}), bf16[8,24,8]{1,2,0:T(8,128)(2,1)S(1)}, u32[]{:S(2)}, u32[]{:S(2)}) async-start(bf16[8,24,8]{1,2,0:T(8,128)(2,1)} %copy.35), calls=%async_computation.4 | async-start | bytes 32768 | tf_op jit(solution)/shard_map/all_to_all | solution.py:53
  174.0 1.1 fusion.18
  175.1 3.7 %all-to-all-done.3 = bf16[8,24,8]{1,2,0:T(8,128)(2,1)S(1)} async-done(((bf16[8,24,8]{1,2,0:T(8,128)(2,1)}), bf16[8,24,8]{1,2,0:T(8,128)(2,1)S(1)}, u32[]{:S(2)}, u32[]{:S(2)}) %all-to-all-start.3) | async-done | bytes 3104 | tf_op jit(solution)/shard_map/all_to_all | solution.py:53
  178.8 0.7 squeeze.19
  179.5 2.0 %reduce-scatter.2.cloned.1.call-done = bf16[24,4096]{1,0:T(8,128)(2,1)} async-done(((bf16[192,4096]{1,0:T(8,128)(2,1)}), bf16[24,4096]{1,0:T(8,128)(2,1)}) %reduce-scatter.2.cloned.1.call-update) | async-done | bytes 196624 | tf_op jit(solution)/shard_map/reduce_scatter | solution.py:39
  (1 shorter events, 0.0 us)
Async XLA Ops:
  7.2 12.1 %copy-start = (bf16[24,8,1024]{2,1,0:T(8,128)(2,1)S(1)}, bf16[24,8,1024]{2,1,0:T(8,128)(2,1)}, u32[]{:S(2)}) copy-start(bf16[24,8,1024]{2,1,0:T(8,128)(2,1)} %param.9) | copy-start | bytes 1179652
  7.2 75.6 %all-gather.3.cloned.1.call-start = ((), (), s32[]{:S(2)}) async-start(), calls=%async_computation.5 | async-start | bytes 6488064 | tf_op jit(solution)/shard_map/all_gather | solution.py:19
  20.5 11.7 %all-to-all-start.2 = ((bf16[8,24,1024]{2,1,0:T(8,128)(2,1)}), bf16[8,24,1024]{2,1,0:T(8,128)(2,1)S(1)}, u32[]{:S(2)}, u32[]{:S(2)}) async-start(bf16[8,24,1024]{2,1,0:T(8,128)(2,1)} %copy.33), calls=%async_computation.2 | async-start | bytes 786432 | tf_op jit(solution)/shard_map/all_to_all | solution.py:26
  23.9 96.6 %all-gather.5.cloned.1.call-start = ((), (), s32[]{:S(2)}) async-start(), calls=%async_computation.6 | async-start | bytes 1966080 | tf_op jit(solution)/shard_map/all_gather | solution.py:27
  32.2 0.7 copy-start.1
  32.9 148.6 %reduce-scatter.2.cloned.1.call-start = ((), (), s32[]{:S(2)}) async-start(), calls=%async_computation.7 | async-start | bytes 1769472 | tf_op jit(solution)/shard_map/reduce_scatter | solution.py:39
  153.1 15.1 %all-to-all-start = ((bf16[8,2,12288]{2,1,0:T(2,128)(2,1)}), bf16[8,2,12288]{2,1,0:T(2,128)(2,1)S(1)}, u32[]{:S(2)}, u32[]{:S(2)}) async-start(bf16[8,2,12288]{2,1,0:T(2,128)(2,1)} %reshape.24), calls=%async_computation | async-start | bytes 786432 | tf_op jit(solution)/shard_map/all_to_all | solution.py:32
  156.7 8.0 %copy-start.2 = (bf16[768,1024]{1,0:T(8,128)(2,1)S(1)}, bf16[768,1024]{1,0:T(8,128)(2,1)}, u32[]{:S(2)}) copy-start(bf16[768,1024]{1,0:T(8,128)(2,1)} %all-gather.5.cloned.1.call-done) | copy-start | bytes 4718596
  169.8 9.0 %all-to-all-start.3 = ((bf16[8,24,8]{1,2,0:T(8,128)(2,1)}), bf16[8,24,8]{1,2,0:T(8,128)(2,1)S(1)}, u32[]{:S(2)}, u32[]{:S(2)}) async-start(bf16[8,24,8]{1,2,0:T(8,128)(2,1)} %copy.35), calls=%async_computation.4 | async-start | bytes 32768 | tf_op jit(solution)/shard_map/all_to_all | solution.py:53
Sparse Core Ops, SparseCore 0:
  10.9 71.8 all-gather.2
  84.9 35.5 all-gather.4
  144.2 37.2 reduce-scatter.1
where the time goes:
time: 189 us; the launch traced here: 188 us
  waiting for transfers between devices  81.9 us (43%)
  matrix products  60.7 us (32%)
  between operations  13.8 us (7%)
  starting transfers between devices  11.4 us (6%)
  blocking collectives  10.2 us (5%)
  local copies, waits for them, and re-layouts  7.07 us (4%)
  other arithmetic  2.92 us (2%)
    all_gather x1, waiting for transfers between devices, on_device(): rows_all = lax.all_gather(trunk, ('dp', 'expert'), axis=0, tiled=True)  49.8 us
    dot_general x1, matrix products, on_device(): pre = jnp.dot(rows_all, first, preferred_element_type=F32)  20.2 us
    all_gather x1, waiting for transfers between devices, on_device(): d_output_all = lax.all_gather(d_output, 'dp', axis=0, tiled=True)  17.5 us
    dot_general x1, matrix products, on_device(): lax.dot_general(d_pre_here, first, (((1,), (1,)), ((), ())), preferred_el...  12.8 us
    dot_general x1, matrix products, on_device(): lax.dot_general(d_output_all, second, (((1,), (1,)), ((), ())), preferred...  10.8 us
    all_to_all x1, blocking collectives, on_device(): lax.all_to_all(gate_here.T[None], 'expert', split_axis=1, concat_axis=0,...  10.2 us
    all_to_all x1, waiting for transfers between devices, on_device(): lax.all_to_all(d_out_each, 'expert', split_axis=0, concat_axis=1, tiled=T...  8.19 us
    dot_general x1, matrix products, on_device(): lax.dot_general(columns, d_pre, (((0,), (0,)), ((), ())), preferred_eleme...  7.99 us
  transfers between devices with their start and end apart: 6, of which 5 were waited for; matrix products, arithmetic and copies ran while one was open for 25% of the time, Pallas kernels for 0%

commit v1 on v0

--- a/solution.py
+++ b/solution.py
@@ -16,7 +16,12 @@
     depth = first.shape[0] // n_dp
     units = second.shape[0] // n_dp
     group = gate_here.shape[1]
-    rows_all = lax.all_gather(trunk, ("dp", "expert"), axis=0, tiled=True)
+    rows_all = jnp.concatenate(
+        lax.all_to_all(
+            jnp.stack([trunk] * lax.axis_size(("dp", "expert"))), ("dp", "expert"), 0, 0
+        ),
+        axis=0,
+    )
     gates_each = lax.all_to_all(
         gate_here.T[None], "expert", split_axis=1, concat_axis=0, tiled=True
     )

time: 189 us -> 291 us (1.54)
  waiting for transfers between devices: 81.9 us -> 170 us
  blocking collectives: 10.2 us -> 21.6 us
    all_to_all x1, waiting for transfers between devices: 8.19 us -> 163 us  [on_device(): lax.all_to_all(jnp.stack([trunk] * lax.axis_size(('dp', 'expert'))), ('dp...]
    all_gather x1 -> x0, waiting for transfers between devices: 49.8 us -> none  [on_device(): rows_all = lax.all_gather(trunk, ('dp', 'expert'), axis=0, tiled=True)]
    all_gather x1, waiting for transfers between devices: 17.5 us -> 0.01 us  [on_device(): d_output_all = lax.all_gather(d_output, 'dp', axis=0, tiled=True)]
    all_to_all x0 -> x1, blocking collectives: none -> 11.4 us  [on_device(): lax.all_to_all(d_out_each, 'expert', split_axis=0, concat_axis=1, tiled=T...]
    another operation x0 -> x1, local copies, waits for them, and re-layouts: none -> 4.33 us  [on_device(): jnp.stack([trunk] * lax.axis_size(('dp', 'expert')))]
  transfers between devices with their start and end apart: 6 -> 5, of which waited for: 5 -> 3; matrix products, arithmetic and copies ran while one was open for 25% -> 15% of each run, Pallas kernels for 0% -> 0%
where the time goes in v1:
time: 291 us
  waiting for transfers between devices  170 us (58%)
  matrix products  60.7 us (21%)
  blocking collectives  21.6 us (7%)
  between operations  14.2 us (5%)
  starting transfers between devices  11.7 us (4%)
  local copies, waits for them, and re-layouts  9.95 us (3%)
  other arithmetic  2.92 us (1%)
    all_to_all x1, waiting for transfers between devices, on_device(): lax.all_to_all(jnp.stack([trunk] * lax.axis_size(('dp', 'expert'))), ('dp...  163 us
    dot_general x1, matrix products, on_device(): pre = jnp.dot(rows_all, first, preferred_element_type=F32)  20.2 us
    dot_general x1, matrix products, on_device(): lax.dot_general(d_pre_here, first, (((1,), (1,)), ((), ())), preferred_el...  12.9 us
    all_to_all x1, blocking collectives, on_device(): lax.all_to_all(d_out_each, 'expert', split_axis=0, concat_axis=1, tiled=T...  11.4 us
    dot_general x1, matrix products, on_device(): lax.dot_general(d_output_all, second, (((1,), (1,)), ((), ())), preferred...  10.8 us
    all_to_all x1, blocking collectives, on_device(): lax.all_to_all(gate_here.T[None], 'expert', split_axis=1, concat_axis=0,...  10.2 us
    dot_general x1, matrix products, on_device(): lax.dot_general(columns, d_pre, (((0,), (0,)), ((), ())), preferred_eleme...  7.99 us
  transfers between devices with their start and end apart: 5, of which 3 were waited for; matrix products, arithmetic and copies ran while one was open for 15% of the time, Pallas kernels for 0%

profile of v1, /device:TPU:0, one launch (start us, length us, event | category | flops | bytes accessed | tf_op | source)
XLA Modules:
  0.0 291.0 jit_solution(3029622097694692427)
XLA Ops:
  7.2 0.0 copy-start
  7.2 0.9 copy.28
  8.1 10.2 %all_to_all.47 = bf16[1,192,8]{2,0,1:T(2,128)(2,1)S(1)} all-to-all(bf16[1,192,8]{2,0,1:T(2,128)(2,1)S(1)} %copy.28), channel_id=1, replica_groups=mesh['expert'=8,'dp'=4] {'expert'}, dimensions={1} | all-to-all | bytes 6144 | tf_op jit(solution)/shard_map/all_to_all | solution.py:25
  18.3 0.1 copy.29
  18.3 0.1 all_to_all.18
  18.4 0.1 copy.32
  18.5 0.0 copy-done
  18.6 0.2 fusion.19
  18.8 0.2 copy.33
  19.0 11.4 %all_to_all.48 = bf16[8,24,1024]{2,1,0:T(8,128)(2,1)} all-to-all(bf16[8,24,1024]{2,1,0:T(8,128)(2,1)S(1)} %copy.33), channel_id=1, replica_groups=mesh['expert'=8,'dp'=4] {'expert'}, dimensions={0} | all-to-all | bytes 786432 | tf_op jit(solution)/shard_map/all_to_all | solution.py:31
  30.4 4.3 %stack.2 = bf16[32,24,4096]{2,1,0:T(8,128)(2,1)} broadcast(bf16[24,4096]{1,0:T(8,128)(2,1)} %param.5), dimensions={1,2} | broadcast | bytes 6488064 | tf_op jit(solution)/shard_map/stack | solution.py:21
  34.8 4.1 %all-to-all-start = ((bf16[32,24,4096]{2,1,0:T(8,128)(2,1)}), bf16[32,24,4096]{2,1,0:T(8,128)(2,1)}, u32[]{:S(2)}, u32[]{:S(2)}) async-start(bf16[32,24,4096]{2,1,0:T(8,128)(2,1)} %stack.2), calls=%async_computation | async-start | bytes 12582912 | tf_op jit(solution)/shard_map/all_to_all | solution.py:20
  38.9 0.0 all-gather.2.cloned.1.call-start
  38.9 0.7 all-gather.2.cloned.1.call-update
  39.6 0.0 reduce-scatter.2.cloned.1.call-start
  39.6 163.3 %all-to-all-done = bf16[32,24,4096]{2,1,0:T(8,128)(2,1)} async-done(((bf16[32,24,4096]{2,1,0:T(8,128)(2,1)}), bf16[32,24,4096]{2,1,0:T(8,128)(2,1)}, u32[]{:S(2)}, u32[]{:S(2)}) %all-to-all-start) | async-done | bytes 6291488 | tf_op jit(solution)/shard_map/all_to_all | solution.py:20
  203.0 20.2 %fusion.2 = f32[768,2048]{1,0:T(8,128)} fusion(bf16[768,4096]{1,0:T(8,128)(2,1)} %bitcast, bf16[1,4096,2048]{2,1,0:T(8,128)(2,1)} %param.6), kind=kOutput, calls=%fused_computation.2 | convolution fusion | flops 12884901888 | bytes 29360128 | tf_op jit(solution)/shard_map/dot_general | solution.py:33
  223.2 0.0 all-gather.2.cloned.1.call-done
  223.2 10.8 %multiply_convert_fusion = bf16[768,2048]{1,0:T(8,128)(2,1)} fusion(f32[768,2048]{1,0:T(8,128)} %fusion.2, bf16[768,1024]{1,0:T(8,128)(2,1)} %all-gather.2.cloned.1.call-done, bf16[1,2048,1024]{2,1,0:T(8,128)(2,1)} %param.7), kind=kOutput, calls=%fused_computation.4 | convolution fusion | flops 3235381248 | bytes 15204352 | tf_op jit(solution)/shard_map/dot_general | solution.py:38
  233.9 12.9 %fusion.4 = bf16[192,4096]{1,0:T(8,128)(2,1)} fusion(bf16[1,4096,2048]{2,1,0:T(8,128)(2,1)} %param.6, bf16[768,2048]{1,0:T(8,128)(2,1)} %multiply_convert_fusion, s32[]{:T(128)S(6)} %select_n.10), kind=kOutput, calls=%fused_computation.5 | convolution fusion | flops 3222011904 | bytes 19136516 | tf_op jit(solution)/shard_map/dot_general | solution.py:45
  246.8 0.0 reduce-scatter.2.cloned.1.call-update
  246.8 3.7 %fusion.20 = bf16[1,192,1024]{2,1,0:T(8,128)(2,1)S(1)} fusion(bf16[1,2048,1024]{2,1,0:T(8,128)(2,1)} %param.7, f32[768,2048]{1,0:T(8,128)} %fusion.2, s32[]{:T(128)S(6)} %select_n.10), kind=kOutput, calls=%fused_computation.21 | convolution fusion | flops 807469056 | bytes 6160388 | tf_op jit(solution)/shard_map/dot_general | solution.py:36
  250.5 0.6 copy.43
  251.1 0.5 broadcast.11
  251.6 2.9 %reduce = bf16[192,1024]{1,0:T(8,128)(2,1)S(1)} reduce(bf16[192,1,1024]{2,1,0:T(2,128)(2,1)S(1)} %bitcast.57, bf16[]{:T(256)} %broadcast.11), dimensions={1}, to_apply=%bitcast.56.reduce_sub_computation | reduce | bytes 786434
  254.6 1.2 reshape.30
  255.8 3.5 %all-to-all-start.1 = ((bf16[8,2,12288]{2,1,0:T(2,128)(2,1)}), bf16[8,2,12288]{2,1,0:T(2,128)(2,1)S(1)}, u32[]{:S(2)}, u32[]{:S(2)}) async-start(bf16[8,2,12288]{2,1,0:T(2,128)(2,1)} %reshape.30), calls=%async_computation.1 | async-start | bytes 786432 | tf_op jit(solution)/shard_map/all_to_all | solution.py:37
  259.3 0.0 copy-start.1
  259.3 8.0 %convert_bitcast_fusion = bf16[1,1024,2048]{2,1,0:T(8,128)(2,1)} fusion(bf16[768,2048]{1,0:T(8,128)(2,1)} %multiply_convert_fusion, bf16[768,4096]{1,0:T(8,128)(2,1)} %bitcast, s32[]{:T(128)S(6)} %select_n.11), kind=kOutput, calls=%fused_computation.10 | convolution fusion | flops 3223322624 | bytes 8912900 | tf_op jit(solution)/shard_map/dot_general | solution.py:61
  267.3 0.0 copy-done.1
  267.3 3.5 %fusion.14 = bf16[1,512,1024]{2,1,0:T(8,128)(2,1)} fusion(bf16[768,1024]{1,0:T(8,128)(2,1)S(1)} %copy-done.1, f32[768,2048]{1,0:T(8,128)} %fusion.2, s32[]{:T(128)S(6)} %select_n.12), kind=kOutput, calls=%fused_computation.15 | convolution fusion | flops 807796736 | bytes 4194308 | tf_op jit(solution)/shard_map/dot_general | solution.py:66
  270.7 0.0 all-to-all-done.1
  270.7 0.4 reshape.31
  271.1 0.1 copy.37
  271.2 0.4 fusion.23
  271.6 0.7 copy.35
  272.3 4.1 %all-to-all-start.4 = ((bf16[8,24,8]{1,2,0:T(8,128)(2,1)}), bf16[8,24,8]{1,2,0:T(8,128)(2,1)S(1)}, u32[]{:S(2)}, u32[]{:S(2)}) async-start(bf16[8,24,8]{1,2,0:T(8,128)(2,1)} %copy.35), calls=%async_computation.5 | async-start | bytes 32768 | tf_op jit(solution)/shard_map/all_to_all | solution.py:58
  276.4 1.1 fusion.18
  277.6 3.7 %all-to-all-done.4 = bf16[8,24,8]{1,2,0:T(8,128)(2,1)S(1)} async-done(((bf16[8,24,8]{1,2,0:T(8,128)(2,1)}), bf16[8,24,8]{1,2,0:T(8,128)(2,1)S(1)}, u32[]{:S(2)}, u32[]{:S(2)}) %all-to-all-start.4) | async-done | bytes 3104 | tf_op jit(solution)/shard_map/all_to_all | solution.py:58
  281.3 0.7 squeeze.19
  282.0 2.2 reduce-scatter.2.cloned.1.call-done
  (1 shorter events, 0.0 us)
Async XLA Ops:
  7.2 11.4 %copy-start = (bf16[24,8,1024]{2,1,0:T(8,128)(2,1)S(1)}, bf16[24,8,1024]{2,1,0:T(8,128)(2,1)}, u32[]{:S(2)}) copy-start(bf16[24,8,1024]{2,1,0:T(8,128)(2,1)} %param.9) | copy-start | bytes 1179652
  34.8 168.2 %all-to-all-start = ((bf16[32,24,4096]{2,1,0:T(8,128)(2,1)}), bf16[32,24,4096]{2,1,0:T(8,128)(2,1)}, u32[]{:S(2)}, u32[]{:S(2)}) async-start(bf16[32,24,4096]{2,1,0:T(8,128)(2,1)} %stack.2), calls=%async_computation | async-start | bytes 12582912 | tf_op jit(solution)/shard_map/all_to_all | solution.py:20
  38.9 184.3 %all-gather.2.cloned.1.call-start = ((), (), s32[]{:S(2)}) async-start(), calls=%async_computation.6 | async-start | bytes 1966080 | tf_op jit(solution)/shard_map/all_gather | solution.py:32
  39.6 244.6 %reduce-scatter.2.cloned.1.call-start = ((), (), s32[]{:S(2)}) async-start(), calls=%async_computation.7 | async-start | bytes 1769472 | tf_op jit(solution)/shard_map/reduce_scatter | solution.py:44
  255.8 14.9 %all-to-all-start.1 = ((bf16[8,2,12288]{2,1,0:T(2,128)(2,1)}), bf16[8,2,12288]{2,1,0:T(2,128)(2,1)S(1)}, u32[]{:S(2)}, u32[]{:S(2)}) async-start(bf16[8,2,12288]{2,1,0:T(2,128)(2,1)} %reshape.30), calls=%async_computation.1 | async-start | bytes 786432 | tf_op jit(solution)/shard_map/all_to_all | solution.py:37
  259.3 8.0 %copy-start.1 = (bf16[768,1024]{1,0:T(8,128)(2,1)S(1)}, bf16[768,1024]{1,0:T(8,128)(2,1)}, u32[]{:S(2)}) copy-start(bf16[768,1024]{1,0:T(8,128)(2,1)} %all-gather.2.cloned.1.call-done) | copy-start | bytes 4718596
  272.3 9.0 %all-to-all-start.4 = ((bf16[8,24,8]{1,2,0:T(8,128)(2,1)}), bf16[8,24,8]{1,2,0:T(8,128)(2,1)S(1)}, u32[]{:S(2)}, u32[]{:S(2)}) async-start(bf16[8,24,8]{1,2,0:T(8,128)(2,1)} %copy.35), calls=%async_computation.5 | async-start | bytes 32768 | tf_op jit(solution)/shard_map/all_to_all | solution.py:58
Sparse Core Ops, SparseCore 0:
  41.2 76.1 all-gather.1
  247.0 37.1 reduce-scatter.1
